TPU v7x, 32 devices: a whole 2x2x4 slice. The times are simulated.
32 devices in a mesh: row: 4 (over y, x), col: 8 (over z, core).
Axes of the slice: x: 2, y: 2, z: 4, core: 2. Of those that a mesh axis runs over, the one named last changes fastest.
Arguments:
- right_side: float32 [512, 128], P('row'), may hold values from -6 to 6
- factor_window: float32 [512, 512], P('row', 'col'), may hold values from -0.1875 to 0.1875
- diag_inverse: float32 [512, 128], P('row'), as said below
- phase_cov: bfloat16 [512, 16384], P('col', 'row'), may hold values from -0.25 to 0.25
Outputs:
- basis: float32 [32, 512, 128], P('row', 'col')
- solved: float32 [512, 128], P('col')
Inputs may be any that keep to these rules, and one draw needn't show every extreme that they name: `diag_inverse`: each block of 128 rows is a lower triangular matrix with a diagonal between 0.5 and 2.
All inputs are finite; a program needn't handle non-finite values.
Results may differ from a plain program's by a relative error of at most 0.0043.
Values sent between devices are 32-bit elements; how exact they have to be, the bound alone decides.
A program may use at most 64 MiB of HBM per device.

v0:
```python
import jax
import jax.numpy as jnp
from jax import lax
from jax.sharding import PartitionSpec as P

TILE_ROWS = 512


def from_root(block, axis, owner):
    block = jnp.where(lax.axis_index(axis) == owner, block, jnp.zeros_like(block))
    return lax.psum(block, axis)


def tile_basis(lower, tile):
    return jax.scipy.linalg.solve_triangular(lower, tile.T, lower=True).T


def finish_tiles(gram, tiles):
    lower = jnp.linalg.cholesky(gram)
    return jax.vmap(tile_basis)(lower, tiles)


def local(right_side, factor_window, diag_inverse, phase_cov):
    row_count = lax.axis_size("row")
    col_count = lax.axis_size("col")
    col_index = lax.axis_index("col")
    block_rows = right_side.shape[0]
    rank_width = right_side.shape[1]
    col_width = factor_window.shape[1]
    col_ratio = col_count // row_count
    row_offset = col_index % col_ratio * col_width
    owner_block = col_index // col_ratio
    partial_value = jnp.zeros((block_rows, rank_width), jnp.float32)
    own_solved = jnp.zeros((col_width, rank_width), jnp.float32)
    for block_index in range(row_count):
        summed = lax.psum(partial_value, "col")
        remaining = right_side - summed
        solved_full = jnp.dot(
            diag_inverse,
            remaining,
            precision=lax.Precision.HIGHEST,
            preferred_element_type=jnp.float32,
        )
        received = from_root(solved_full, "row", block_index)
        column_piece = lax.dynamic_slice_in_dim(received, row_offset, col_width, 0)
        owns_block = owner_block == block_index
        own_solved = jnp.where(owns_block, column_piece, own_solved)
        partial_value = lax.cond(
            owns_block,
            lambda running: running
            + jnp.dot(
                factor_window,
                column_piece,
                precision=lax.Precision.HIGHEST,
                preferred_element_type=jnp.float32,
            ),
            lambda running: running,
            partial_value,
        )
    solved_low = own_solved.astype(jnp.bfloat16)
    tile_count = phase_cov.shape[1] // TILE_ROWS
    cov_tiles = phase_cov.reshape(col_width, tile_count, TILE_ROWS)
    whole_tiles = lax.psum_scatter(
        jnp.einsum("kts,kr->tsr", cov_tiles, solved_low, preferred_element_type=jnp.float32),
        "col",
        scatter_dimension=0,
        tiled=True,
    )
    gram = jnp.einsum("tsr,tsq->trq", whole_tiles, whole_tiles, precision=lax.Precision.HIGHEST)
    tile_bases = finish_tiles(gram, whole_tiles)
    basis = lax.all_to_all(tile_bases, "col", split_axis=1, concat_axis=0, tiled=True)
    return (basis, own_solved)


def solution(mesh):
    in_specs = (P("row", None), P("row", "col"), P("row", None), P("col", "row"))
    out_specs = (P("row", "col", None), P("col", None))
    return jax.shard_map(local, mesh=mesh, in_specs=in_specs, out_specs=out_specs, check_vma=False)
```

profile of v0, /device:TPU:0, one launch (start us, length us, event | category | flops | bytes accessed | tf_op | source)
XLA Modules:
  0.0 444.9 jit_solution(12275134099939349102)
XLA Ops:
  7.2 0.8 copy-done
  8.0 1.7 convolution_select_fusion.3
  9.8 46.2 %all-reduce.8.cloned.1.call-done = f32[128,128]{1,0:T(8,128)} async-done(((f32[128,128]{1,0:T(8,128)}), f32[128,128]{1,0:T(8,128)}) %all-reduce.8.cloned.1.call-update) | async-done | bytes 65552 | tf_op jit(solution)/shard_map/psum | solution.py:11
  56.0 0.8 constant_dynamic-slice_fusion.2
  56.8 1.0 conditional.3
  56.8 1.0 fusion.16
  58.5 55.1 %all-reduce.10.cloned.1.call-done = f32[128,128]{1,0:T(8,128)} async-done(((f32[128,128]{1,0:T(8,128)}), f32[128,128]{1,0:T(8,128)}) %all-reduce.10.cloned.1.call-update) | async-done | bytes 65552 | tf_op jit(solution)/shard_map/psum | solution.py:36
  113.6 1.7 fusion.2
  115.4 42.0 %all-reduce.12.cloned.1.call-done = f32[128,128]{1,0:T(8,128)} async-done(((f32[128,128]{1,0:T(8,128)}), f32[128,128]{1,0:T(8,128)}) %all-reduce.12.cloned.1.call-update) | async-done | bytes 65552 | tf_op jit(solution)/shard_map/psum | solution.py:11
  157.4 0.8 constant_dynamic-slice_fusion.1
  158.2 56.6 %all-reduce.14.cloned.1.call-done = f32[128,128]{1,0:T(8,128)} async-done(((f32[128,128]{1,0:T(8,128)}), f32[128,128]{1,0:T(8,128)}) %all-reduce.14.cloned.1.call-update) | async-done | bytes 65552 | tf_op jit(solution)/shard_map/psum | solution.py:36
  214.9 1.7 fusion.1
  216.7 41.8 %all-reduce.16.cloned.1.call-done = f32[128,128]{1,0:T(8,128)} async-done(((f32[128,128]{1,0:T(8,128)}), f32[128,128]{1,0:T(8,128)}) %all-reduce.16.cloned.1.call-update) | async-done | bytes 65552 | tf_op jit(solution)/shard_map/psum | solution.py:11
  259.3 56.6 %all-reduce.18.cloned.1.call-done = f32[128,128]{1,0:T(8,128)} async-done(((f32[128,128]{1,0:T(8,128)}), f32[128,128]{1,0:T(8,128)}) %all-reduce.18.cloned.1.call-update) | async-done | bytes 65552 | tf_op jit(solution)/shard_map/psum | solution.py:36
  316.0 1.7 fusion
  317.8 42.6 %all-reduce.20.cloned.1.call-done = f32[128,128]{1,0:T(8,128)} async-done(((f32[128,128]{1,0:T(8,128)}), f32[128,128]{1,0:T(8,128)}) %all-reduce.20.cloned.1.call-update) | async-done | bytes 65552 | tf_op jit(solution)/shard_map/psum | solution.py:11
  360.3 0.8 select_select_fusion.1
  361.2 1.8 convolution_bitcast_fusion
  363.0 36.4 %reduce-scatter.2.cloned.1.call-done = f32[1,512,128]{1,2,0:T(8,128)} async-done(((f32[8,512,128]{1,2,0:T(8,128)}), f32[1,512,128]{1,2,0:T(8,128)}) %reduce-scatter.2.cloned.1.call-update) | async-done | bytes 262160 | tf_op jit(solution)/shard_map/reduce_scatter | solution.py:63
  399.3 1.4 fusion.6
  400.9 11.7 %custom-call.8 = f32[1,128,128]{2,1,0:T(8,128)S(1)} custom-call(f32[1,128,128]{2,1,0:T(8,128)S(1)} %fusion.9), custom_call_target="Cholesky" | custom-call | tf_op jit(solution)/shard_map/jit(cholesky)/cholesky | solution.py:19
  413.9 9.8 %custom-call.9 = f32[1,1,128,128]{2,3,1,0:T(8,128)S(1)} custom-call(f32[1,1,128,128]{3,2,1,0:T(8,128)S(1)} %fusion.8), custom_call_target="InvertDiagBlocksLowerTriangular" | custom-call | tf_op jit(solution)/shard_map/vmap(jit(_solve_triangular))/triangular_solve | solution.py:15
  423.7 1.4 convolution_bitcast_fusion.1
  425.2 12.1 %all_to_all.12 = f32[1,512,128]{2,0,1:T(1,128)S(1)} all-to-all(f32[1,512,128]{2,0,1:T(1,128)S(1)} %copy.38), channel_id=1, replica_groups=mesh['row'=4,'col'=8] {'col'}, dimensions={1} | all-to-all | bytes 524288 | tf_op jit(solution)/shard_map/all_to_all | solution.py:71
  (33 shorter events, 4.1 us)
Async XLA Ops:
  7.2 0.8 copy-start
  7.2 354.0 %copy-start.2 = (bf16[64,4096]{1,0:T(8,128)(2,1)S(1)}, bf16[64,4096]{1,0:T(8,128)(2,1)}, u32[]{:S(2)}) copy-start(bf16[64,4096]{1,0:T(8,128)(2,1)} %param.13) | copy-start | bytes 1572868
  7.2 48.8 %all-reduce.8.cloned.1.call-start = ((), (), s32[]{:S(2)}) async-start(), calls=%async_computation.2 | async-start | bytes 131072 | tf_op jit(solution)/shard_map/psum | solution.py:11
  9.7 103.9 %all-reduce.10.cloned.1.call-start = ((), (), s32[]{:S(2)}) async-start(), calls=%async_computation.3 | async-start | bytes 131072 | tf_op jit(solution)/shard_map/psum | solution.py:36
  57.8 0.6 copy-start.1
  58.5 98.9 %all-reduce.12.cloned.1.call-start = ((), (), s32[]{:S(2)}) async-start(), calls=%async_computation.4 | async-start | bytes 131072 | tf_op jit(solution)/shard_map/psum | solution.py:11
  115.4 99.5 %all-reduce.14.cloned.1.call-start = ((), (), s32[]{:S(2)}) async-start(), calls=%async_computation.5 | async-start | bytes 131072 | tf_op jit(solution)/shard_map/psum | solution.py:36
  158.2 100.3 %all-reduce.16.cloned.1.call-start = ((), (), s32[]{:S(2)}) async-start(), calls=%async_computation.6 | async-start | bytes 131072 | tf_op jit(solution)/shard_map/psum | solution.py:11
  216.6 99.4 %all-reduce.18.cloned.1.call-start = ((), (), s32[]{:S(2)}) async-start(), calls=%async_computation.7 | async-start | bytes 131072 | tf_op jit(solution)/shard_map/psum | solution.py:36
  259.3 101.0 %all-reduce.20.cloned.1.call-start = ((), (), s32[]{:S(2)}) async-start(), calls=%async_computation.8 | async-start | bytes 131072 | tf_op jit(solution)/shard_map/psum | solution.py:11
  317.7 81.6 %reduce-scatter.2.cloned.1.call-start = ((), (), s32[]{:S(2)}) async-start(), calls=%async_computation.9 | async-start | bytes 2359296 | tf_op jit(solution)/shard_map/reduce_scatter | solution.py:63
  361.1 1.8 copy-start.3
Sparse Core Ops, SparseCore 0:
  11.4 44.5 all-reduce.7
  58.9 54.6 all-reduce.9
  116.5 40.8 all-reduce.11
  160.1 54.6 all-reduce.13
  217.6 40.8 all-reduce.15
  261.2 54.6 all-reduce.17
  319.4 40.8 all-reduce.19
  363.1 36.2 reduce-scatter.1
where the time goes:
time: 446 us; the launch traced here: 445 us
  waiting for transfers between devices  377 us (85%)
  other arithmetic  23.7 us (5%)
  between operations  14.3 us (3%)
  matrix products  12.4 us (3%)
  blocking collectives  12.1 us (3%)
  local copies, waits for them, and re-layouts  4.6 us (1%)
    psum x4, waiting for transfers between devices, from_root(): return lax.psum(block, axis)  173 us
    psum x3, waiting for transfers between devices, local(): summed = lax.psum(partial_value, 'col')  168 us
    reduce_scatter x1, waiting for transfers between devices, local(): lax.psum_scatter(jnp.einsum('kts,kr->tsr', cov_tiles, solved_low, preferr...  36.4 us
    another operation x3, other arithmetic, finish_tiles(): lower = jnp.linalg.cholesky(gram)  12.4 us
    all_to_all x1, blocking collectives, local(): lax.all_to_all(tile_bases, 'col', split_axis=1, concat_axis=0, tiled=True)  12.1 us
    another operation x2, other arithmetic, tile_basis(): return jax.scipy.linalg.solve_triangular(lower, tile.T, lower=True).T  10.5 us
  transfers between devices with their start and end apart: 8, of which 8 were waited for; matrix products, arithmetic and copies ran while one was open for 0% of the time, Pallas kernels for 0%

commit v1 on v0

--- a/solution.py
+++ b/solution.py
@@ -33,7 +33,9 @@
     partial_value = jnp.zeros((block_rows, rank_width), jnp.float32)
     own_solved = jnp.zeros((col_width, rank_width), jnp.float32)
     for block_index in range(row_count):
-        summed = lax.psum(partial_value, "col")
+        summed = partial_value
+        for hop in (1, 2, 4):
+            summed = summed + lax.ppermute(summed, "col", [(dev, dev ^ hop) for dev in range(8)])
         remaining = right_side - summed
         solved_full = jnp.dot(
             diag_inverse,

time: 446 us -> 315 us (0.71)
  waiting for transfers between devices: 377 us -> 232 us
  starting transfers between devices: 0.33 us -> 18.2 us
    psum x3 -> x0, waiting for transfers between devices: 168 us -> none  [local(): summed = lax.psum(partial_value, 'col')]
    ppermute x0 -> x12, waiting for transfers between devices: none -> 28.3 us  [local(): lax.ppermute(summed, 'col', [(dev, dev ^ hop) for dev in range(8)])]
    ppermute x0 -> x12, starting transfers between devices: none -> 18 us  [local(): lax.ppermute(summed, 'col', [(dev, dev ^ hop) for dev in range(8)])]
    psum x4, waiting for transfers between devices: 173 us -> 168 us  [from_root(): return lax.psum(block, axis)]
  transfers between devices with their start and end apart: 8 -> 17, of which waited for: 8 -> 17; matrix products, arithmetic and copies ran while one was open for 0% -> 0% of each run, Pallas kernels for 0% -> 0%
where the time goes in v1:
time: 315 us; the launch traced here: 314 us
  waiting for transfers between devices  232 us (74%)
  other arithmetic  23.7 us (8%)
  starting transfers between devices  18.2 us (6%)
  between operations  14 us (4%)
  blocking collectives  12.1 us (4%)
  matrix products  9.88 us (3%)
  local copies, waits for them, and re-layouts  4.3 us (1%)
    psum x4, waiting for transfers between devices, from_root(): return lax.psum(block, axis)  168 us
    reduce_scatter x1, waiting for transfers between devices, local(): lax.psum_scatter(jnp.einsum('kts,kr->tsr', cov_tiles, solved_low, preferr...  36.1 us
    ppermute x12, waiting for transfers between devices, local(): lax.ppermute(summed, 'col', [(dev, dev ^ hop) for dev in range(8)])  28.3 us
    ppermute x12, starting transfers between devices, local(): lax.ppermute(summed, 'col', [(dev, dev ^ hop) for dev in range(8)])  18 us
    another operation x3, other arithmetic, finish_tiles(): lower = jnp.linalg.cholesky(gram)  12.4 us
    all_to_all x1, blocking collectives, local(): lax.all_to_all(tile_bases, 'col', split_axis=1, concat_axis=0, tiled=True)  12.1 us
    another operation x2, other arithmetic, tile_basis(): return jax.scipy.linalg.solve_triangular(lower, tile.T, lower=True).T  10.5 us
  transfers between devices with their start and end apart: 17, of which 17 were waited for; matrix products, arithmetic and copies ran while one was open for 0% of the time, Pallas kernels for 0%

profile of v1, /device:TPU:0, one launch (start us, length us, event | category | flops | bytes accessed | tf_op | source)
XLA Modules:
  0.0 314.4 jit_solution(10559324621815543435)
XLA Ops:
  8.7 2.9 collective-permute-start.1
  11.6 2.4 collective-permute-done.1
  14.1 2.9 collective-permute-start.2
  20.3 44.0 %all-reduce.5.cloned.1.call-done = f32[128,128]{1,0:T(8,128)} async-done(((f32[128,128]{1,0:T(8,128)}), f32[128,128]{1,0:T(8,128)}) %all-reduce.5.cloned.1.call-update) | async-done | bytes 65552 | tf_op jit(solution)/shard_map/psum | solution.py:11
  68.0 3.8 %collective-permute-done.4 = f32[128,128]{1,0:T(8,128)S(1)} collective-permute-done((f32[128,128]{1,0:T(8,128)S(1)}, f32[128,128]{1,0:T(8,128)S(1)}, u32[]{:S(2)}, u32[]{:S(2)}) %collective-permute-start.4) | collective-permute-done | bytes 65568 | tf_op jit(solution)/shard_map/ppermute | solution.py:38
  71.9 1.4 collective-permute-start.5
  73.3 4.4 %collective-permute-done.5 = f32[128,128]{1,0:T(8,128)S(1)} collective-permute-done((f32[128,128]{1,0:T(8,128)S(1)}, f32[128,128]{1,0:T(8,128)S(1)}, u32[]{:S(2)}, u32[]{:S(2)}) %collective-permute-start.5) | collective-permute-done | bytes 65568 | tf_op jit(solution)/shard_map/ppermute | solution.py:38
  77.7 1.7 fusion.2
  79.5 41.0 %all-reduce.7.cloned.1.call-done = f32[128,128]{1,0:T(8,128)} async-done(((f32[128,128]{1,0:T(8,128)}), f32[128,128]{1,0:T(8,128)}) %all-reduce.7.cloned.1.call-update) | async-done | bytes 65552 | tf_op jit(solution)/shard_map/psum | solution.py:11
  122.6 2.7 collective-permute-start.7
  125.2 2.4 collective-permute-done.7
  127.7 1.7 collective-permute-start.8
  129.4 3.5 %collective-permute-done.8 = f32[128,128]{1,0:T(8,128)S(1)} collective-permute-done((f32[128,128]{1,0:T(8,128)S(1)}, f32[128,128]{1,0:T(8,128)S(1)}, u32[]{:S(2)}, u32[]{:S(2)}) %collective-permute-start.8) | collective-permute-done | bytes 65568 | tf_op jit(solution)/shard_map/ppermute | solution.py:38
  133.8 41.9 %all-reduce.9.cloned.1.call-done = f32[128,128]{1,0:T(8,128)} async-done(((f32[128,128]{1,0:T(8,128)}), f32[128,128]{1,0:T(8,128)}) %all-reduce.9.cloned.1.call-update) | async-done | bytes 65552 | tf_op jit(solution)/shard_map/psum | solution.py:11
  177.7 1.6 collective-permute-start.10
  179.3 2.8 collective-permute-done.10
  182.1 3.6 %collective-permute-start.11 = (f32[128,128]{1,0:T(8,128)S(1)}, f32[128,128]{1,0:T(8,128)S(1)}, u32[]{:S(2)}, u32[]{:S(2)}) collective-permute-start(f32[128,128]{1,0:T(8,128)S(1)} %add.83), channel_id=1, source_target_pairs={{0,4},{1,5},{2,6},{3,7},{4,0},{5,1},{6,2},{7,3},{8,12},{9,13},{10,... | collective-permute-start | bytes 196616 | tf_op jit(solution)/shard_map/ppermute | solution.py:38
  185.7 2.9 collective-permute-done.11
  189.5 40.8 %all-reduce.11.cloned.1.call-done = f32[128,128]{1,0:T(8,128)} async-done(((f32[128,128]{1,0:T(8,128)}), f32[128,128]{1,0:T(8,128)}) %all-reduce.11.cloned.1.call-update) | async-done | bytes 65552 | tf_op jit(solution)/shard_map/psum | solution.py:11
  231.2 1.8 convolution_bitcast_fusion
  233.0 36.1 %reduce-scatter.2.cloned.1.call-done = f32[1,512,128]{1,2,0:T(8,128)} async-done(((f32[8,512,128]{1,2,0:T(8,128)}), f32[1,512,128]{1,2,0:T(8,128)}) %reduce-scatter.2.cloned.1.call-update) | async-done | bytes 262160 | tf_op jit(solution)/shard_map/reduce_scatter | solution.py:65
  270.7 11.7 %custom-call.8 = f32[1,128,128]{2,1,0:T(8,128)S(1)} custom-call(f32[1,128,128]{2,1,0:T(8,128)S(1)} %fusion.10), custom_call_target="Cholesky" | custom-call | tf_op jit(solution)/shard_map/jit(cholesky)/cholesky | solution.py:19
  283.7 9.8 %custom-call.9 = f32[1,1,128,128]{2,3,1,0:T(8,128)S(1)} custom-call(f32[1,1,128,128]{3,2,1,0:T(8,128)S(1)} %fusion.9), custom_call_target="InvertDiagBlocksLowerTriangular" | custom-call | tf_op jit(solution)/shard_map/vmap(jit(_solve_triangular))/triangular_solve | solution.py:15
  295.0 12.1 %all_to_all.12 = f32[1,512,128]{2,0,1:T(1,128)S(1)} all-to-all(f32[1,512,128]{2,0,1:T(1,128)S(1)} %copy.53), channel_id=1, replica_groups=mesh['row'=4,'col'=8] {'col'}, dimensions={1} | all-to-all | bytes 524288 | tf_op jit(solution)/shard_map/all_to_all | solution.py:73
  (61 shorter events, 21.4 us)
Async XLA Ops:
  7.2 12.2 %copy-start = (f32[128,128]{1,0:T(8,128)S(1)}, f32[128,128]{1,0:T(8,128)}, u32[]{:S(2)}) copy-start(f32[128,128]{1,0:T(8,128)} %param.12) | copy-start | bytes 196612
  7.2 125.7 %copy-start.1 = (f32[128,128]{1,0:T(8,128)S(1)}, f32[128,128]{1,0:T(8,128)}, u32[]{:S(2)}) copy-start(f32[128,128]{1,0:T(8,128)} %param.10) | copy-start | bytes 196612
  7.2 57.1 %all-reduce.5.cloned.1.call-start = ((), (), s32[]{:S(2)}) async-start(), calls=%async_computation.2 | async-start | bytes 131072 | tf_op jit(solution)/shard_map/psum | solution.py:11
  7.3 223.9 %copy-start.2 = (bf16[64,4096]{1,0:T(8,128)(2,1)S(1)}, bf16[64,4096]{1,0:T(8,128)(2,1)}, u32[]{:S(2)}) copy-start(bf16[64,4096]{1,0:T(8,128)(2,1)} %param.13) | copy-start | bytes 1572868
  7.3 1.5 collective-permute-start
  8.7 5.3 %collective-permute-start.1 = (f32[128,128]{0,1:T(8,128)S(1)}, f32[128,128]{0,1:T(8,128)S(1)}, u32[]{:S(2)}, u32[]{:S(2)}) collective-permute-start(f32[128,128]{0,1:T(8,128)S(1)} %collective-permute-done), channel_id=1, source_target_pairs={{0,2},{1,3},{2,0},{3,1},{4,6},{5,7},{6,4},{7,5},{8,10},{9,11},{10,... | collective-permute-start | bytes 196616 | tf_op jit(solution)/shard_map/ppermute | solution.py:38
  14.1 5.3 %collective-permute-start.2 = (f32[128,128]{0,1:T(8,128)S(1)}, f32[128,128]{0,1:T(8,128)S(1)}, u32[]{:S(2)}, u32[]{:S(2)}) collective-permute-start(f32[128,128]{0,1:T(8,128)S(1)} %add.72), channel_id=1, source_target_pairs={{0,4},{1,5},{2,6},{3,7},{4,0},{5,1},{6,2},{7,3},{8,12},{9,13},{10,... | collective-permute-start | bytes 196616 | tf_op jit(solution)/shard_map/ppermute | solution.py:38
  20.2 100.2 %all-reduce.7.cloned.1.call-start = ((), (), s32[]{:S(2)}) async-start(), calls=%async_computation.3 | async-start | bytes 131072 | tf_op jit(solution)/shard_map/psum | solution.py:11
  64.3 166.0 %copy-start.4 = (f32[128,128]{1,0:T(8,128)S(1)}, f32[128,128]{1,0:T(8,128)}, u32[]{:S(2)}) copy-start(f32[128,128]{1,0:T(8,128)} %all-reduce.5.cloned.1.call-done) | copy-start | bytes 196612
  66.2 1.3 collective-permute-start.3
  67.5 4.3 %collective-permute-start.4 = (f32[128,128]{1,0:T(8,128)S(1)}, f32[128,128]{1,0:T(8,128)S(1)}, u32[]{:S(2)}, u32[]{:S(2)}) collective-permute-start(f32[128,128]{1,0:T(8,128)S(1)} %add.76), channel_id=1, source_target_pairs={{0,2},{1,3},{2,0},{3,1},{4,6},{5,7},{6,4},{7,5},{8,10},{9,11},{10,... | collective-permute-start | bytes 196616 | tf_op jit(solution)/shard_map/ppermute | solution.py:38
  71.9 5.8 %collective-permute-start.5 = (f32[128,128]{1,0:T(8,128)S(1)}, f32[128,128]{1,0:T(8,128)S(1)}, u32[]{:S(2)}, u32[]{:S(2)}) collective-permute-start(f32[128,128]{1,0:T(8,128)S(1)} %add.77), channel_id=1, source_target_pairs={{0,4},{1,5},{2,6},{3,7},{4,0},{5,1},{6,2},{7,3},{8,12},{9,13},{10,... | collective-permute-start | bytes 196616 | tf_op jit(solution)/shard_map/ppermute | solution.py:38
  79.4 96.3 %all-reduce.9.cloned.1.call-start = ((), (), s32[]{:S(2)}) async-start(), calls=%async_computation.4 | async-start | bytes 131072 | tf_op jit(solution)/shard_map/psum | solution.py:11
  120.5 109.9 %copy-start.5 = (f32[128,128]{1,0:T(8,128)S(1)}, f32[128,128]{1,0:T(8,128)}, u32[]{:S(2)}) copy-start(f32[128,128]{1,0:T(8,128)} %all-reduce.7.cloned.1.call-done) | copy-start | bytes 196612
  121.3 1.3 collective-permute-start.6
  122.6 5.1 %collective-permute-start.7 = (f32[128,128]{1,0:T(8,128)S(1)}, f32[128,128]{1,0:T(8,128)S(1)}, u32[]{:S(2)}, u32[]{:S(2)}) collective-permute-start(f32[128,128]{1,0:T(8,128)S(1)} %add.79), channel_id=1, source_target_pairs={{0,2},{1,3},{2,0},{3,1},{4,6},{5,7},{6,4},{7,5},{8,10},{9,11},{10,... | collective-permute-start | bytes 196616 | tf_op jit(solution)/shard_map/ppermute | solution.py:38
  127.7 5.3 %collective-permute-start.8 = (f32[128,128]{1,0:T(8,128)S(1)}, f32[128,128]{1,0:T(8,128)S(1)}, u32[]{:S(2)}, u32[]{:S(2)}) collective-permute-start(f32[128,128]{1,0:T(8,128)S(1)} %add.80), channel_id=1, source_target_pairs={{0,4},{1,5},{2,6},{3,7},{4,0},{5,1},{6,2},{7,3},{8,12},{9,13},{10,... | collective-permute-start | bytes 196616 | tf_op jit(solution)/shard_map/ppermute | solution.py:38
  133.8 96.5 %all-reduce.11.cloned.1.call-start = ((), (), s32[]{:S(2)}) async-start(), calls=%async_computation.5 | async-start | bytes 131072 | tf_op jit(solution)/shard_map/psum | solution.py:11
  176.5 1.3 collective-permute-start.9
  177.7 4.3 %collective-permute-start.10 = (f32[128,128]{1,0:T(8,128)S(1)}, f32[128,128]{1,0:T(8,128)S(1)}, u32[]{:S(2)}, u32[]{:S(2)}) collective-permute-start(f32[128,128]{1,0:T(8,128)S(1)} %add.82), channel_id=1, source_target_pairs={{0,2},{1,3},{2,0},{3,1},{4,6},{5,7},{6,4},{7,5},{8,10},{9,11},{10,... | collective-permute-start | bytes 196616 | tf_op jit(solution)/shard_map/ppermute | solution.py:38
  182.1 6.5 %collective-permute-start.11 = (f32[128,128]{1,0:T(8,128)S(1)}, f32[128,128]{1,0:T(8,128)S(1)}, u32[]{:S(2)}, u32[]{:S(2)}) collective-permute-start(f32[128,128]{1,0:T(8,128)S(1)} %add.83), channel_id=1, source_target_pairs={{0,4},{1,5},{2,6},{3,7},{4,0},{5,1},{6,2},{7,3},{8,12},{9,13},{10,... | collective-permute-start | bytes 196616 | tf_op jit(solution)/shard_map/ppermute | solution.py:38
  189.5 79.7 %reduce-scatter.2.cloned.1.call-start = ((), (), s32[]{:S(2)}) async-start(), calls=%async_computation.6 | async-start | bytes 2359296 | tf_op jit(solution)/shard_map/reduce_scatter | solution.py:65
  231.1 1.8 copy-start.3
Sparse Core Ops, SparseCore 0:
  20.4 43.8 all-reduce.4
  79.5 40.8 all-reduce.6
  133.9 41.7 all-reduce.8
  189.6 40.6 all-reduce.10
  233.1 35.9 reduce-scatter.1
